TPU v7x, 128 devices: a whole 4x4x4 slice. The times are simulated.
128 devices in a mesh: sec: 4 (over x), op: 32 (over z, y, core).
Axes of the slice: x: 4, y: 4, z: 4, core: 2. Of those that a mesh axis runs over, the one named last changes fastest.
Arguments:
- wavefunction: bfloat16 [4, 1024, 1024], P('sec'), may hold values from -6 to 6
- left_operator: bfloat16 [128, 4, 1024, 1024], P('op', 'sec'), may hold values from -0.011048543 to 0.35355339
- right_operator: bfloat16 [128, 1024, 1024], P('op'), may hold values from -0.125 to 1.125
- sector_size: int32 [4], replicated, may hold values from 512 to 1024
- term_shift: int32 [128], replicated, may hold values from 0 to 3, as said below
Outputs:
- sigma: float32 [4, 1024, 1024], P('sec', 'op')
- residual: float32 [4, 1024, 1024], P('sec', 'op')
Inputs may be any that keep to these rules, and one draw needn't show every extreme that they name: `term_shift`: among the 4 terms of one index of op (terms g * 4 to g * 4 + 3), the shifts are distinct.
All inputs are finite; a program needn't handle non-finite values.
Results may differ from a plain program's by a relative error of at most 0.0025.
Values may be sent and summed in bfloat16 or wider, within the bound.
A program may use at most 128 MiB of HBM per device.

v0:
```python
import jax
import jax.numpy as jnp
from jax import lax
from jax.sharding import Mesh
from jax.sharding import PartitionSpec as P

OP = ("op_0", "op_1", "op_2")
SEC_OP = ("sec", "op_0", "op_1", "op_2")


def over_axes(x, axes):
    for axis in axes:
        x = lax.psum(x, axis)
    return x


def per_device(wavefunction, left_operator, right_operator, sector_size, term_shift):
    sec_count = lax.axis_size("sec")
    op_count = lax.axis_size(OP)
    sec_index = lax.axis_index("sec")
    op_index = lax.axis_index(OP)
    term_count = left_operator.shape[0]
    sector_rows = wavefunction.shape[1]
    col_count = wavefunction.shape[2]
    row_count = sector_rows // op_count
    positions = jnp.arange(sector_rows, dtype=jnp.int32)
    own_size = sector_size[sec_index]
    masked = wavefunction[0] * (positions < own_size).astype(jnp.bfloat16)[:, None]
    left_image = jnp.einsum(
        "tmn,nk->tmk", left_operator[:, 0], masked, preferred_element_type=jnp.float32
    ).astype(jnp.bfloat16)
    right_image = jnp.einsum(
        "tmk,tkl->tml", left_image, right_operator, preferred_element_type=jnp.float32
    ).astype(jnp.bfloat16)
    local_shifts = lax.dynamic_slice_in_dim(term_shift, op_index * term_count, term_count)
    targets = (sec_index + local_shifts) % sec_count
    routing_onehot = (targets[:, None] == jnp.arange(sec_count, dtype=jnp.int32)[None, :]).astype(
        jnp.bfloat16
    )
    outgoing = jnp.einsum(
        "tn,tmk->nmk", routing_onehot, right_image, preferred_element_type=jnp.float32
    ).astype(jnp.bfloat16)
    blocks = outgoing.reshape(sec_count * op_count, row_count, col_count)
    incoming = lax.all_to_all(blocks, SEC_OP, split_axis=0, concat_axis=0, tiled=True)
    summed = jnp.sum(incoming, axis=0, dtype=jnp.float32)
    global_rows = op_index * row_count + jnp.arange(row_count, dtype=jnp.int32)
    out_mask = (global_rows < own_size).astype(jnp.float32)
    sigma_rows = summed * out_mask[:, None]
    state_rows = lax.dynamic_slice_in_dim(masked, op_index * row_count, row_count, 0).astype(
        jnp.float32
    )
    norm_sum, cross_sum = (
        over_axes(jnp.sum(state_rows * state_rows), SEC_OP),
        over_axes(jnp.sum(state_rows * sigma_rows), SEC_OP),
    )
    energy = cross_sum / norm_sum
    residual_rows = sigma_rows - energy * state_rows
    return (sigma_rows[None], residual_rows[None])


def solution(mesh):
    finer = Mesh(mesh.devices.reshape(mesh.shape["sec"], 4, 4, 2), ("sec", "op_0", "op_1", "op_2"))
    return jax.shard_map(
        per_device,
        mesh=finer,
        in_specs=(P("sec", None, None), P(OP, "sec", None, None), P(OP, None, None), P(), P()),
        out_specs=(P("sec", OP, None), P("sec", OP, None)),
        check_vma=False,
    )
```

profile of v0, /device:TPU:1, one launch (start us, length us, event | category | flops | bytes accessed | tf_op | source)
XLA Modules:
  0.0 231.8 jit_solution(6037880737334125754)
XLA Ops:
  0.6 1.2 dynamic_slice.10
  1.9 0.6 fusion.16
  2.5 12.7 %fusion.5 = bf16[1024,4,1024]{2,0,1:T(8,128)(2,1)S(1)} fusion(bf16[4,1,1024,1024]{3,2,1,0:T(8,128)(2,1)} %param.6, bf16[1,1024,1024]{2,1,0:T(8,128)(2,1)} %param.5, bf16[1024]{0:T(1024)(128)(2,1)S(1)} %fusion.16), kind=kOutput, calls=%fused_computation.8 | convolution fusion | flops 8598323200 | bytes 18876416 | tf_op jit(solution)/shard_map/tmn,nk->tmk/dot_general | solution.py:29
  15.2 0.0 copy-start
  15.2 22.8 %copy.19 = bf16[1024,4,1024]{2,1,0:T(4,128)(2,1)} copy(bf16[1024,4,1024]{2,0,1:T(8,128)(2,1)S(1)} %fusion.5) | data formatting | bytes 16777216
  38.0 0.0 copy-done
  38.0 0.1 and_select_fusion
  38.1 14.9 %fusion.3 = bf16[4,1024,1024]{2,1,0:T(8,128)(2,1)S(1)} fusion(bf16[4,1024,1024]{2,1,0:T(8,128)(2,1)} %param.7, bf16[4,1024,1024]{1,0,2:T(4,128)(2,1)} %bitcast.24), kind=kOutput, calls=%fused_computation.6 | convolution fusion | flops 8589934592 | bytes 25165824 | tf_op jit(solution)/shard_map/tmk,tkl->tml/dot_general | solution.py:32
  53.0 7.5 %fusion.8 = bf16[4,1024,1024]{2,0,1:T(4,128)(2,1)} fusion(bf16[4,1024,1024]{2,1,0:T(8,128)(2,1)S(1)} %fusion.3, s32[4]{0:T(128)S(1)} %and_select_fusion), kind=kOutput, calls=%fused_computation.9 | convolution fusion | flops 37748752 | bytes 16777232 | tf_op jit(solution)/shard_map/tn,tmk->nmk/dot_general | solution.py:40
  60.4 9.5 %copy.7 = bf16[4,1024,1024]{2,1,0:T(8,128)(2,1)} copy(bf16[4,1024,1024]{2,0,1:T(4,128)(2,1)} %fusion.8) | data formatting | bytes 16777216 | tf_op jit(solution)/shard_map/convert_element_type | solution.py:42
  69.9 12.0 %all-to-all-start = ((bf16[128,32,1024]{2,1,0:T(8,128)(2,1)}), bf16[128,32,1024]{2,1,0:T(8,128)(2,1)}, u32[]{:S(2)}, u32[]{:S(2)}) async-start(bf16[128,32,1024]{2,1,0:T(8,128)(2,1)} %bitcast.23), calls=%async_computation | async-start | bytes 16777216 | tf_op jit(solution)/shard_map/all_to_all | solution.py:44
  81.9 0.1 dynamic-slice
  81.9 0.6 compare_convert_fusion
  82.6 105.4 %all-to-all-done = bf16[128,32,1024]{2,1,0:T(8,128)(2,1)} async-done(((bf16[128,32,1024]{2,1,0:T(8,128)(2,1)}), bf16[128,32,1024]{2,1,0:T(8,128)(2,1)}, u32[]{:S(2)}, u32[]{:S(2)}) %all-to-all-start) | async-done | bytes 8388640 | tf_op jit(solution)/shard_map/all_to_all | solution.py:44
  188.0 5.2 %convert_reduce_fusion = f32[32,1024]{1,0:T(8,128)S(1)} fusion(bf16[128,32,1024]{2,1,0:T(8,128)(2,1)} %all-to-all-done), kind=kLoop, calls=%fused_computation.1 | loop fusion | flops 8355840 | bytes 8519680 | tf_op jit(solution)/shard_map/reduce_sum | solution.py:45
  193.2 0.7 bitcast_multiply_fusion
  194.0 1.6 fusion.13
  195.5 6.7 %all-reduce.2 = (f32[]{:T(128)}, f32[]{:T(128)}) all-reduce(f32[]{:T(128)} %get-tuple-element.3, f32[]{:T(128)} %get-tuple-element.2), channel_id=1, replica_groups=mesh['sec'=4,'op_0'=4,'op_1'=4,'op_2'=2] {'sec'}, use_global_device_ids=true, to_apply=%region_2.3 | all-reduce | flops 2 | bytes 16 | tf_op jit(solution)/shard_map/psum | solution.py:13
  202.2 7.9 %all-reduce.1 = (f32[]{:T(128)}, f32[]{:T(128)}) all-reduce(f32[]{:T(128)} %get-tuple-element.8, f32[]{:T(128)} %get-tuple-element.9), channel_id=1, replica_groups=mesh['sec'=4,'op_0'=4,'op_1'=4,'op_2'=2] {'op_0'}, use_global_device_ids=true, to_apply=%region_3.4 | all-reduce | flops 2 | bytes 16 | tf_op jit(solution)/shard_map/psum | solution.py:13
  210.1 9.3 %all-reduce = (f32[]{:T(128)}, f32[]{:T(128)}) all-reduce(f32[]{:T(128)} %get-tuple-element.6, f32[]{:T(128)} %get-tuple-element.7), channel_id=1, replica_groups=mesh['sec'=4,'op_0'=4,'op_1'=4,'op_2'=2] {'op_1'}, use_global_device_ids=true, to_apply=%region_4.5 | all-reduce | flops 2 | bytes 16 | tf_op jit(solution)/shard_map/psum | solution.py:13
  219.4 9.5 %all-reduce.3 = (f32[]{:T(128)}, f32[]{:T(128)}) all-reduce(f32[]{:T(128)} %get-tuple-element.4, f32[]{:T(128)} %get-tuple-element.5), channel_id=1, replica_groups=mesh['sec'=4,'op_0'=4,'op_1'=4,'op_2'=2] {'op_2'}, use_global_device_ids=true, to_apply=%region_5.6 | all-reduce | flops 2 | bytes 16 | tf_op jit(solution)/shard_map/psum | solution.py:13
  230.2 1.6 fusion.15
Async XLA Ops:
  15.2 22.8 %copy-start = (s32[128]{0:T(128)S(1)}, s32[128]{0:T(128)}, u32[]{:S(2)}) copy-start(s32[128]{0:T(128)} %param.9) | copy-start | bytes 1540
  69.9 118.1 %all-to-all-start = ((bf16[128,32,1024]{2,1,0:T(8,128)(2,1)}), bf16[128,32,1024]{2,1,0:T(8,128)(2,1)}, u32[]{:S(2)}, u32[]{:S(2)}) async-start(bf16[128,32,1024]{2,1,0:T(8,128)(2,1)} %bitcast.23), calls=%async_computation | async-start | bytes 16777216 | tf_op jit(solution)/shard_map/all_to_all | solution.py:44
where the time goes:
time: 232 us
  waiting for transfers between devices  105 us (45%)
  matrix products  35 us (15%)
  local copies, waits for them, and re-layouts  33.5 us (14%)
  blocking collectives  33.4 us (14%)
  starting transfers between devices  12 us (5%)
  other arithmetic  10.5 us (5%)
    all_to_all x1, waiting for transfers between devices, per_device(): lax.all_to_all(blocks, SEC_OP, split_axis=0, concat_axis=0, tiled=True)  105 us
    psum x4, blocking collectives, over_axes(): x = lax.psum(x, axis)  33.4 us
    unnamed x3, local copies, waits for them, and re-layouts  22.8 us
    dot_general x1, matrix products, per_device(): jnp.einsum('tmk,tkl->tml', left_image, right_operator, preferred_element_...  14.9 us
    dot_general x1, matrix products, per_device(): jnp.einsum('tmn,nk->tmk', left_operator[:, 0], masked, preferred_element_...  12.7 us
    all_to_all x1, starting transfers between devices, per_device(): lax.all_to_all(blocks, SEC_OP, split_axis=0, concat_axis=0, tiled=True)  12 us
    convert_element_type x1, local copies, waits for them, and re-layouts, per_device(): outgoing = jnp.einsum('tn,tmk->nmk', routing_onehot, right_image, preferr...  9.46 us
    dot_general x1, matrix products, per_device(): jnp.einsum('tn,tmk->nmk', routing_onehot, right_image, preferred_element_...  7.45 us
  transfers between devices with their start and end apart: 1, of which 1 were waited for; matrix products, arithmetic and copies ran while one was open for 0% of the time, Pallas kernels for 0%

commit v1 on v0

--- a/solution.py
+++ b/solution.py
@@ -10,7 +10,7 @@
 
 def over_axes(x, axes):
     for axis in axes:
-        x = lax.psum(x, axis)
+        x = jnp.sum(lax.all_gather(x, axis), axis=0)
     return x
 
 

time: 232 us -> 248 us (1.069)
  local copies, waits for them, and re-layouts: 33.5 us -> 47.1 us
  other arithmetic: 10.5 us -> 15.6 us
  blocking collectives: 33.4 us -> 30.7 us
    psum x4 -> x0, blocking collectives: 33.4 us -> none  [over_axes(): x = lax.psum(x, axis)]
    unnamed x0 -> x4, blocking collectives: none -> 30.7 us
    unnamed x3 -> x31, local copies, waits for them, and re-layouts: 22.8 us -> 36.3 us
    reduce_sum x0 -> x8, other arithmetic: none -> 5.13 us  [over_axes(): x = jnp.sum(lax.all_gather(x, axis), axis=0)]
  transfers between devices with their start and end apart: 1 -> 1, of which waited for: 1 -> 1; matrix products, arithmetic and copies ran while one was open for 0% -> 1% of each run, Pallas kernels for 0% -> 0%
where the time goes in v1:
time: 248 us; the launch traced here: 247 us
  waiting for transfers between devices  105 us (42%)
  local copies, waits for them, and re-layouts  47.1 us (19%)
  matrix products  35 us (14%)
  blocking collectives  30.7 us (12%)
  other arithmetic  15.6 us (6%)
  starting transfers between devices  12 us (5%)
    all_to_all x1, waiting for transfers between devices, per_device(): lax.all_to_all(blocks, SEC_OP, split_axis=0, concat_axis=0, tiled=True)  105 us
    unnamed x31, local copies, waits for them, and re-layouts  36.3 us
    unnamed x4, blocking collectives  30.7 us
    dot_general x1, matrix products, per_device(): jnp.einsum('tmk,tkl->tml', left_image, right_operator, preferred_element_...  14.9 us
    dot_general x1, matrix products, per_device(): jnp.einsum('tmn,nk->tmk', left_operator[:, 0], masked, preferred_element_...  12.7 us
    all_to_all x1, starting transfers between devices, per_device(): lax.all_to_all(blocks, SEC_OP, split_axis=0, concat_axis=0, tiled=True)  12 us
    convert_element_type x1, local copies, waits for them, and re-layouts, per_device(): outgoing = jnp.einsum('tn,tmk->nmk', routing_onehot, right_image, preferr...  9.46 us
    dot_general x1, matrix products, per_device(): jnp.einsum('tn,tmk->nmk', routing_onehot, right_image, preferred_element_...  7.45 us
  transfers between devices with their start and end apart: 1, of which 1 were waited for; matrix products, arithmetic and copies ran while one was open for 1% of the time, Pallas kernels for 0%

profile of v1, /device:TPU:1, one launch (start us, length us, event | category | flops | bytes accessed | tf_op | source)
XLA Modules:
  0.0 247.3 jit_solution(12263125900290284244)
XLA Ops:
  0.6 1.2 dynamic_slice.10
  1.9 0.6 fusion.16
  2.5 12.7 %fusion.5 = bf16[1024,4,1024]{2,0,1:T(8,128)(2,1)S(1)} fusion(bf16[4,1,1024,1024]{3,2,1,0:T(8,128)(2,1)} %param.6, bf16[1,1024,1024]{2,1,0:T(8,128)(2,1)} %param.5, bf16[1024]{0:T(1024)(128)(2,1)S(1)} %fusion.16), kind=kOutput, calls=%fused_computation.8 | convolution fusion | flops 8598323200 | bytes 18876416 | tf_op jit(solution)/shard_map/tmn,nk->tmk/dot_general | solution.py:29
  15.2 0.0 copy-start
  15.2 22.8 %copy.19 = bf16[1024,4,1024]{2,1,0:T(4,128)(2,1)} copy(bf16[1024,4,1024]{2,0,1:T(8,128)(2,1)S(1)} %fusion.5) | data formatting | bytes 16777216
  38.0 0.0 copy-done
  38.0 0.1 and_select_fusion
  38.1 14.9 %fusion.3 = bf16[4,1024,1024]{2,1,0:T(8,128)(2,1)S(1)} fusion(bf16[4,1024,1024]{2,1,0:T(8,128)(2,1)} %param.7, bf16[4,1024,1024]{1,0,2:T(4,128)(2,1)} %bitcast.36), kind=kOutput, calls=%fused_computation.6 | convolution fusion | flops 8589934592 | bytes 25165824 | tf_op jit(solution)/shard_map/tmk,tkl->tml/dot_general | solution.py:32
  53.0 7.5 %fusion.8 = bf16[4,1024,1024]{2,0,1:T(4,128)(2,1)} fusion(bf16[4,1024,1024]{2,1,0:T(8,128)(2,1)S(1)} %fusion.3, s32[4]{0:T(128)S(1)} %and_select_fusion), kind=kOutput, calls=%fused_computation.9 | convolution fusion | flops 37748752 | bytes 16777232 | tf_op jit(solution)/shard_map/tn,tmk->nmk/dot_general | solution.py:40
  60.4 9.5 %copy.7 = bf16[4,1024,1024]{2,1,0:T(8,128)(2,1)} copy(bf16[4,1024,1024]{2,0,1:T(4,128)(2,1)} %fusion.8) | data formatting | bytes 16777216 | tf_op jit(solution)/shard_map/convert_element_type | solution.py:42
  69.9 0.0 copy-start.4
  69.9 12.0 %all-to-all-start = ((bf16[128,32,1024]{2,1,0:T(8,128)(2,1)}), bf16[128,32,1024]{2,1,0:T(8,128)(2,1)}, u32[]{:S(2)}, u32[]{:S(2)}) async-start(bf16[128,32,1024]{2,1,0:T(8,128)(2,1)} %bitcast.35), calls=%async_computation | async-start | bytes 16777216 | tf_op jit(solution)/shard_map/all_to_all | solution.py:44
  81.9 0.0 copy-start.3
  81.9 0.0 copy-start.2
  81.9 0.0 copy-start.1
  81.9 0.1 dynamic-slice.8
  82.0 0.0 copy-done.4
  82.0 0.6 dynamic-slice
  82.6 0.6 compare_convert_fusion
  83.2 104.8 %all-to-all-done = bf16[128,32,1024]{2,1,0:T(8,128)(2,1)} async-done(((bf16[128,32,1024]{2,1,0:T(8,128)(2,1)}), bf16[128,32,1024]{2,1,0:T(8,128)(2,1)}, u32[]{:S(2)}, u32[]{:S(2)}) %all-to-all-start) | async-done | bytes 8388640 | tf_op jit(solution)/shard_map/all_to_all | solution.py:44
  188.0 5.2 %convert_reduce_fusion = f32[32,1024]{1,0:T(8,128)S(1)} fusion(bf16[128,32,1024]{2,1,0:T(8,128)(2,1)} %all-to-all-done), kind=kLoop, calls=%fused_computation.1 | loop fusion | flops 8355840 | bytes 8519680 | tf_op jit(solution)/shard_map/reduce_sum | solution.py:45
  193.2 1.6 fusion.13
  194.8 1.3 dynamic-update-slice
  196.1 1.3 dynamic-update-slice.4
  197.4 0.0 copy-done.3
  197.4 0.6 dynamic-slice.1
  198.0 6.0 %all-reduce.10 = (f32[4]{0:T(128)S(1)}, f32[4]{0:T(128)S(1)}) all-reduce(f32[4]{0:T(128)S(1)} %dynamic-update-slice, f32[4]{0:T(128)S(1)} %dynamic-update-slice.4), channel_id=1, replica_groups=mesh['sec'=4,'op_0'=4,'op_1'=4,'op_2'=2] {'sec'}, use_global_device_ids=true, to_apply=%add | all-reduce | flops 8 | bytes 64
  204.0 0.7 reduce_sum.109
  204.7 0.6 reduce_sum.104
  205.3 1.4 dynamic-update-slice.5
  206.7 1.4 dynamic-update-slice.1
  208.1 0.0 copy-done.2
  208.1 0.6 dynamic-slice.2
  208.7 7.3 %all-reduce.9 = (f32[4]{0:T(128)S(1)}, f32[4]{0:T(128)S(1)}) all-reduce(f32[4]{0:T(128)S(1)} %dynamic-update-slice.1, f32[4]{0:T(128)S(1)} %dynamic-update-slice.5), channel_id=1, replica_groups=mesh['sec'=4,'op_0'=4,'op_1'=4,'op_2'=2] {'op_0'}, use_global_device_ids=true, to_apply=%add.1 | all-reduce | flops 8 | bytes 64
  216.0 0.7 reduce_sum.110
  216.7 0.6 reduce_sum.105
  217.3 1.4 dynamic-update-slice.6
  218.7 1.4 dynamic-update-slice.2
  220.1 0.0 copy-done.1
  220.1 0.6 dynamic-slice.3
  220.7 8.6 %all-reduce.8 = (f32[4]{0:T(128)S(1)}, f32[4]{0:T(128)S(1)}) all-reduce(f32[4]{0:T(128)S(1)} %dynamic-update-slice.2, f32[4]{0:T(128)S(1)} %dynamic-update-slice.6), channel_id=1, replica_groups=mesh['sec'=4,'op_0'=4,'op_1'=4,'op_2'=2] {'op_1'}, use_global_device_ids=true, to_apply=%add.2 | all-reduce | flops 8 | bytes 64
  229.3 0.7 reduce_sum.111
  230.0 0.6 reduce_sum.106
  230.6 1.4 dynamic-update-slice.7
  232.0 1.4 dynamic-update-slice.3
  233.4 0.7 bitcast_multiply_fusion
  234.2 8.8 %all-reduce.11 = (f32[2]{0:T(128)S(1)}, f32[2]{0:T(128)S(1)}) all-reduce(f32[2]{0:T(128)S(1)} %dynamic-update-slice.3, f32[2]{0:T(128)S(1)} %dynamic-update-slice.7), channel_id=1, replica_groups=mesh['sec'=4,'op_0'=4,'op_1'=4,'op_2'=2] {'op_2'}, use_global_device_ids=true, to_apply=%add.3 | all-reduce | flops 4 | bytes 32
  243.0 0.6 reduce_sum.107
  243.6 0.7 reduce_sum.112
  245.7 1.6 fusion.15
  (8 shorter events, 0.0 us)
Async XLA Ops:
  15.2 22.8 %copy-start = (s32[128]{0:T(128)S(1)}, s32[128]{0:T(128)}, u32[]{:S(2)}) copy-start(s32[128]{0:T(128)} %param.9) | copy-start | bytes 1540
  69.9 12.1 %copy-start.4 = (u32[128]{0:T(128)S(1)}, u32[128]{0:T(128)}, u32[]{:S(2)}) copy-start(u32[128]{0:T(128)} %constant.48) | copy-start | bytes 1540
  69.9 118.1 %all-to-all-start = ((bf16[128,32,1024]{2,1,0:T(8,128)(2,1)}), bf16[128,32,1024]{2,1,0:T(8,128)(2,1)}, u32[]{:S(2)}, u32[]{:S(2)}) async-start(bf16[128,32,1024]{2,1,0:T(8,128)(2,1)} %bitcast.35), calls=%async_computation | async-start | bytes 16777216 | tf_op jit(solution)/shard_map/all_to_all | solution.py:44
  81.9 115.6 %copy-start.3 = (u32[128]{0:T(128)S(1)}, u32[128]{0:T(128)}, u32[]{:S(2)}) copy-start(u32[128]{0:T(128)} %constant.53) | copy-start | bytes 1540
  81.9 126.3 %copy-start.2 = (u32[128]{0:T(128)S(1)}, u32[128]{0:T(128)}, u32[]{:S(2)}) copy-start(u32[128]{0:T(128)} %constant.58) | copy-start | bytes 1540
  81.9 138.2 %copy-start.1 = (u32[128]{0:T(128)S(1)}, u32[128]{0:T(128)}, u32[]{:S(2)}) copy-start(u32[128]{0:T(128)} %constant.63) | copy-start | bytes 1540
